TPU v7x, 32 devices: a whole 2x2x4 slice. The times are simulated.
32 devices in a mesh: gx: 4 (over y, x), gy: 4 (over z), ga: 2 (over core).
Axes of the slice: x: 2, y: 2, z: 4, core: 2. Of those that a mesh axis runs over, the one named last changes fastest.
Arguments:
- fields: float32 [5, 16, 64, 1024], P(None, 'ga', 'gx', 'gy'), may hold values from -6 to 6
- stiffness: float32 [16, 64, 1024], P('ga', 'gx', 'gy'), may hold values from 0.25 to 4
- lift_weight: float32 [5, 32], replicated, may hold values from -2.5 to 2.5
- lift_bias: float32 [32], replicated, may hold values from -3 to 3
- mix_weight: bfloat16 [32, 32], replicated, may hold values from -0.5 to 0.5
- spectral_weight: float32 [8, 32, 32, 32, 128], P('ga', 'gy', None, 'gx'), may hold values from -0.48 to 0.48
- output_bias: float32 [32], replicated, may hold values from -3 to 3
Outputs:
- layer_out: bfloat16 [16, 32, 32, 512], P('ga', None, 'gx', 'gy')
All inputs are finite; a program needn't handle non-finite values.
Results may differ from a plain program's by a relative error of at most 0.01.
Values may be sent and summed in bfloat16 or wider, within the bound.
A program may use at most 128 MiB of HBM per device.

v0:
```python
import math
import jax
import jax.numpy as jnp
from jax import lax
from jax.sharding import PartitionSpec as P

STEPS = 3
MX = 32
MY = 64
MZ = 8
courant_half = 0.1
smooth_half = 0.15
mean_flow = (0.3, -0.2, 0.1)
highest = lax.Precision.HIGHEST


def padded_2(block, sides, width):
    for axis, dim in sides:
        count = lax.axis_size(axis)
        forward = [(i, i + 1) for i in range(count - 1)]
        forward.append((count - 1, 0))
        backward = [(target, source) for source, target in forward]
        low = lax.ppermute(
            lax.slice_in_dim(block, block.shape[dim] - width, None, axis=dim), axis, forward
        )
        high = lax.ppermute(lax.slice_in_dim(block, 0, width, axis=dim), axis, backward)
        block = jnp.concatenate([low, block, high], axis=dim)
    return block


def step_interior(padded, stiff_part):
    center = padded[:, 1:-1, 1:-1, 1:-1]
    upper_depth = padded[:, 2:, 1:-1, 1:-1]
    lower_depth = padded[:, :-2, 1:-1, 1:-1]
    upper_east = padded[:, 1:-1, 2:, 1:-1]
    lower_east = padded[:, 1:-1, :-2, 1:-1]
    upper_north = padded[:, 1:-1, 1:-1, 2:]
    lower_north = padded[:, 1:-1, 1:-1, :-2]
    slope_depth = upper_depth - lower_depth
    slope_east = upper_east - lower_east
    slope_north = upper_north - lower_north
    curvature = (
        upper_depth
        + lower_depth
        + upper_east
        + lower_east
        + upper_north
        + lower_north
        - 6.0 * center
    )
    transport = mean_flow[0] * slope_east + mean_flow[1] * slope_north + mean_flow[2] * slope_depth
    diverge = slope_east[1] + slope_north[2] + slope_depth[3]
    coupling = jnp.stack(
        [diverge, slope_east[4], slope_north[4], slope_depth[4], stiff_part * diverge]
    )
    return center - courant_half * (transport + coupling) + smooth_half * curvature


def trim(block, margin):
    return block[margin:-margin, margin:-margin, margin:-margin]


def coarsen(fields_now):
    extent = fields_now.shape
    blocks = fields_now.reshape(extent[0], extent[1], extent[2] // 2, 2, extent[3] // 2, 2)
    return 0.25 * (
        blocks[:, :, :, 0, :, 0]
        + blocks[:, :, :, 1, :, 0]
        + blocks[:, :, :, 0, :, 1]
        + blocks[:, :, :, 1, :, 1]
    )


def angles(frequencies, points, length):
    product = jnp.mod(frequencies[:, None] * points[None, :], length)
    return product.astype(jnp.float32) * (2.0 * math.pi / length)


def centered(number):
    return jnp.arange(number, dtype=jnp.int32) - number // 2


def forward_east_table(points, length, mode_count):
    phases = angles(centered(mode_count), points, length)
    factor = 1.0 / math.sqrt(length)
    return (jnp.stack([jnp.cos(phases).T, -jnp.sin(phases).T], axis=1) * factor).astype(
        jnp.bfloat16
    )


def forward_north_table(points, length, mode_count):
    phases = angles(centered(mode_count), points, length)
    factor = 1.0 / math.sqrt(length)
    cosines = jnp.cos(phases).T * factor
    sines = jnp.sin(phases).T * factor
    return jnp.stack(
        [jnp.concatenate([cosines, -sines], axis=1), jnp.concatenate([sines, cosines], axis=1)],
        axis=0,
    )


def inverse_north_table(points, length, mode_count):
    phases = angles(centered(mode_count), points, length)
    factor = 1.0 / math.sqrt(length)
    cosines = jnp.cos(phases) * factor
    sines = jnp.sin(phases) * factor
    return jnp.concatenate(
        [jnp.stack([cosines, sines], axis=1), jnp.stack([-sines, cosines], axis=1)], axis=0
    )


def inverse_east_table(points, length, mode_count):
    phases = angles(centered(mode_count), points, length)
    factor = 1.0 / math.sqrt(length)
    return jnp.stack([jnp.cos(phases) * factor, -jnp.sin(phases) * factor], axis=1)


def forward_depth_blocks(values, points, frequencies, length):
    slot_count = frequencies.shape[0]
    phases = angles(frequencies.reshape(-1), points, length).reshape(
        slot_count, frequencies.shape[1], points.shape[0]
    )
    factor = 1.0 / math.sqrt(length)
    cosines = jnp.cos(phases) * factor
    sines = jnp.sin(phases) * factor
    halfway = values.shape[-1] // 2
    real_in = values[..., :halfway]
    imag_in = values[..., halfway:]
    real_part = jnp.einsum("zcrbn,rkz->rkcbn", real_in, cosines, precision=highest) + jnp.einsum(
        "zcrbn,rkz->rkcbn", imag_in, sines, precision=highest
    )
    imag_part = jnp.einsum("zcrbn,rkz->rkcbn", imag_in, cosines, precision=highest) - jnp.einsum(
        "zcrbn,rkz->rkcbn", real_in, sines, precision=highest
    )
    return jnp.concatenate([real_part, imag_part], axis=-1)


def mix_channels(coeffs, weight):
    halfway = coeffs.shape[-1] // 2
    real_in = coeffs[..., :halfway]
    imag_in = coeffs[..., halfway:]
    weight_real = weight[..., :halfway]
    weight_imag = weight[..., halfway:]
    real_part = jnp.einsum(
        "kcmn,kmcon->komn", real_in, weight_real, precision=highest
    ) - jnp.einsum("kcmn,kmcon->komn", imag_in, weight_imag, precision=highest)
    imag_part = jnp.einsum(
        "kcmn,kmcon->komn", imag_in, weight_real, precision=highest
    ) + jnp.einsum("kcmn,kmcon->komn", real_in, weight_imag, precision=highest)
    return jnp.concatenate([real_part, imag_part], axis=-1)


def inverse_depth(values, frequencies, points, length):
    phases = angles(frequencies, points, length)
    factor = 1.0 / math.sqrt(length)
    cosines = jnp.cos(phases) * factor
    sines = jnp.sin(phases) * factor
    halfway = values.shape[-1] // 2
    real_in = values[..., :halfway]
    imag_in = values[..., halfway:]
    real_part = jnp.einsum("komn,kz->zomn", real_in, cosines, precision=highest) - jnp.einsum(
        "komn,kz->zomn", imag_in, sines, precision=highest
    )
    imag_part = jnp.einsum("komn,kz->zomn", imag_in, cosines, precision=highest) + jnp.einsum(
        "komn,kz->zomn", real_in, sines, precision=highest
    )
    return jnp.concatenate([real_part, imag_part], axis=-1)


def shards(fields, stiffness, lift_weight, lift_bias, mix_weight, spectral_weight, output_bias):
    east_tiles = lax.axis_size("gx")
    north_tiles = lax.axis_size("gy")
    depth_groups = lax.axis_size("ga")
    stacked = jnp.concatenate([fields, stiffness[None]], axis=0)
    padded = padded_2(stacked, (("gx", 2), ("gy", 3), ("ga", 1)), STEPS)
    fields_now = padded[:5]
    for repeat in range(STEPS):
        fields_now = step_interior(fields_now, trim(padded[5], repeat + 1))
    filtered = coarsen(fields_now)
    pre_lift = (
        jnp.einsum("fzxy,fc->zcxy", filtered, lift_weight, precision=highest)
        + lift_bias[None, :, None, None]
    )
    lifted = jax.nn.gelu(pre_lift, approximate=True).astype(jnp.bfloat16)
    depth_local = lifted.shape[0]
    length_east = lifted.shape[2] * east_tiles
    length_north = lifted.shape[3] * north_tiles
    length_depth = depth_local * depth_groups
    east_points = jnp.arange(length_east, dtype=jnp.int32)
    north_points = jnp.arange(length_north, dtype=jnp.int32)
    table_east = forward_east_table(east_points, length_east, MX)
    table_north = forward_north_table(north_points, length_north, MY)
    planes = lax.all_to_all(
        lax.all_to_all(lifted, "gx", split_axis=1, concat_axis=2, tiled=True),
        "gy",
        split_axis=0,
        concat_axis=3,
        tiled=True,
    )
    east_modes = jnp.einsum(
        "zcxy,xpm->zcpmy", planes, table_east, preferred_element_type=jnp.float32
    )
    north_modes = jnp.einsum("zcpmy,pyq->zcmq", east_modes, table_north, precision=highest)
    plane_count = planes.shape[0]
    depth_points = (
        lax.axis_index("ga") * depth_local
        + lax.axis_index("gy") * plane_count
        + jnp.arange(plane_count, dtype=jnp.int32)
    )
    block_east = MX // north_tiles
    block_depth = MZ // depth_groups
    grouped = north_modes.reshape(
        plane_count, north_modes.shape[1], north_tiles, block_east, 2 * MY
    )
    owners = jnp.arange(1 * lax.axis_size(("gy", "ga")), dtype=jnp.int32)
    picked = jnp.take(grouped, owners // depth_groups, axis=2)
    frequencies = (owners % depth_groups)[:, None] * block_depth + jnp.arange(
        block_depth, dtype=jnp.int32
    )[None, :]
    coeffs = lax.psum_scatter(
        forward_depth_blocks(picked, depth_points, frequencies, length_depth).astype(jnp.bfloat16),
        ("gy", "ga"),
        scatter_dimension=0,
        tiled=True,
    ).astype(jnp.float32)[0]
    mixed_modes = mix_channels(lax.all_gather(coeffs, "gx", axis=1, tiled=True), spectral_weight)
    own_frequencies = lax.axis_index("ga") * coeffs.shape[0] + jnp.arange(
        coeffs.shape[0], dtype=jnp.int32
    )
    points = jnp.arange(depth_local * lax.axis_size("ga"), dtype=jnp.int32)
    back_depth = lax.psum_scatter(
        inverse_depth(mixed_modes, own_frequencies, points, length_depth),
        "ga",
        scatter_dimension=0,
        tiled=True,
    )
    back_north = jnp.einsum(
        "zomq,qpy->zompy",
        back_depth,
        inverse_north_table(north_points, length_north, MY),
        precision=highest,
    )
    all_modes = lax.all_to_all(back_north, "gy", split_axis=4, concat_axis=2, tiled=True)
    spectral = jnp.einsum(
        "zompy,mpx->zoxy",
        all_modes,
        inverse_east_table(east_points, length_east, MX),
        precision=highest,
    ).astype(jnp.bfloat16)
    spectral = lax.all_to_all(spectral, "gx", split_axis=2, concat_axis=1, tiled=True)
    direct = jnp.einsum("zcxy,co->zoxy", lifted, mix_weight, preferred_element_type=jnp.float32)
    summed = direct + output_bias[None, :, None, None] + spectral.astype(jnp.float32)
    return jax.nn.gelu(summed, approximate=True).astype(jnp.bfloat16)


def solution(mesh):
    placed = (
        P(None, "ga", "gx", "gy"),
        P("ga", "gx", "gy"),
        P(),
        P(),
        P(),
        P("ga", "gy", None, "gx", None),
        P(),
    )
    return jax.shard_map(
        shards, mesh=mesh, in_specs=placed, out_specs=P("ga", None, "gx", "gy"), check_vma=False
    )
```

profile of v0, /device:TPU:0, one launch (start us, length us, event | category | flops | bytes accessed | tf_op | source)
XLA Modules:
  0.0 479.2 jit_solution(17202555115786274294)
XLA Ops:
  6.5 1.2 fusion.67
  7.8 3.0 collective-permute-start
  12.9 4.0 copy.86
  16.8 4.0 copy.85
  20.8 4.0 copy.87
  24.8 1.4 pad_maximum_fusion.7
  26.2 2.1 collective-permute-start.2
  28.3 2.3 collective-permute-start.3
  30.5 2.7 collective-permute-done.2
  33.5 6.5 %pad_maximum_fusion = f32[6,8,22,262]{2,1,3,0:T(8,128)S(1)} fusion(f32[6,8,22,3]{2,1,3,0:T(8,128)S(1)} %collective-permute-done.3, f32[6,8,3,256]{2,1,3,0:T(8,128)S(1)} %copy-done.2, f32[6,8,16,256]{2,1,3,0:T(8,128)} %copy.86, f32[6,8,3,256]{2,1,3,0:T(8,128)} %copy.85, f32[6,8,22,3]{2,1,3,0:T(8,128)S(1)} %collective-permute-done.2), kind=kLoop, calls=%fused_computation.1 | loop fusion | flops 1106688 | bytes 2213376 | tf_op jit(solution)/shard_map/concatenate | solution.py:27
  40.0 3.1 fusion.167
  43.8 4.0 copy.88
  47.8 2.3 copy.89
  50.6 5.1 %copy.90 = f32[6,8,22,262]{3,2,1,0:T(8,128)S(1)} copy(f32[6,8,22,262]{2,1,3,0:T(8,128)} %copy-done.1) | data formatting | bytes 2213376 | tf_op jit(solution)/shard_map/concatenate | solution.py:27
  55.7 1.3 pad_maximum_fusion.1
  57.0 3.0 slice_subtract_fusion.2
  60.5 4.1 multiply_add_fusion
  64.6 2.5 slice_subtract_fusion.5
  67.5 3.3 multiply_add_fusion.1
  71.9 1.2 multiply_add_fusion.2
  73.1 5.5 %copy.91 = f32[5,8,16,256]{1,3,2,0:T(8,128)} copy(f32[5,8,16,256]{3,2,1,0:T(8,128)S(1)} %multiply_add_fusion.2) | data formatting | bytes 1310720 | tf_op jit(solution)/shard_map/add | solution.py:56
  78.6 10.9 %fusion = f32[5,8,8,1,128,1]{1,5,4,3,2,0:T(1,128)S(1)} fusion(f32[5,8,8,2,128,2]{1,5,4,3,2,0:T(2,128)} %bitcast.187), kind=kLoop, calls=%fused_computation.8 | loop fusion | flops 163840 | bytes 819200 | tf_op jit(solution)/shard_map/mul | solution.py:66
  89.5 1.1 copy.92
  90.7 1.3 fusion.29
  93.0 3.5 all-to-all-start
  96.5 8.4 %all-to-all-done = bf16[8,32,8,128]{3,2,0,1:T(8,128)(2,1)S(1)} async-done(((bf16[8,32,8,128]{3,2,0,1:T(8,128)(2,1)}), bf16[8,32,8,128]{3,2,0,1:T(8,128)(2,1)S(1)}, u32[]{:S(2)}, u32[]{:S(2)}) %all-to-all-start) | async-done | bytes 524320 | tf_op jit(solution)/shard_map/all_to_all | solution.py:194
  105.8 4.4 all-to-all-start.1
  110.7 1.1 fusion.83
  112.2 11.9 %all-to-all-done.1 = bf16[8,8,32,128]{3,2,1,0:T(8,128)(2,1)S(1)} async-done(((bf16[8,8,32,128]{3,2,1,0:T(8,128)(2,1)}), bf16[8,8,32,128]{3,2,1,0:T(8,128)(2,1)S(1)}, u32[]{:S(2)}, u32[]{:S(2)}) %all-to-all-start.1) | async-done | bytes 524320 | tf_op jit(solution)/shard_map/all_to_all | solution.py:193
  125.2 1.8 fusion.19
  128.3 2.4 fusion.56
  130.6 3.0 fusion.52
  133.6 3.3 fusion.14
  136.9 2.5 fusion.15
  141.2 29.5 %reduce-scatter.3.cloned.1.call-done = bf16[1,4,8,8,128]{4,3,2,1,0:T(8,128)(2,1)} async-done(((bf16[8,4,8,8,128]{4,3,2,1,0:T(8,128)(2,1)}), bf16[1,4,8,8,128]{4,3,2,1,0:T(8,128)(2,1)}) %reduce-scatter.3.cloned.1.call-update) | async-done | bytes 65552 | tf_op jit(solution)/shard_map/reduce_scatter | solution.py:220
  171.5 10.2 %all-gather = f32[1,4,32,8,128]{4,3,1,0,2:T(8,128)S(1)} all-gather(f32[1,4,8,8,128]{4,3,1,0,2:T(8,128)S(1)} %copy.100), channel_id=2, replica_groups=mesh['gx'=4,'gy'=4,'ga'=2] {'gx'}, dimensions={2}, use_global_device_ids=true | all-gather | bytes 655360 | tf_op jit(solution)/shard_map/all_gather | solution.py:226
  182.5 1.3 copy-done.3
  183.9 2.4 multiply_reduce_fusion.3
  191.5 5.3 %reduce-scatter.5.cloned.1.call-done = f32[8,8,8,128]{3,0,2,1:T(8,128)} async-done(((f32[16,8,8,128]{3,0,2,1:T(8,128)}), f32[8,8,8,128]{3,0,2,1:T(8,128)}) %reduce-scatter.5.cloned.1.call-update) | async-done | bytes 262160 | tf_op jit(solution)/shard_map/reduce_scatter | solution.py:231
  196.8 2.7 fusion.40
  199.5 23.9 %copy.102 = f32[8,8,8,2,512]{2,3,1,0,4:T(2,128)} copy(f32[8,8,8,2,512]{4,0,3,2,1:T(8,128)S(1)} %fusion.40) | data formatting | bytes 4194304 | tf_op jit(solution)/shard_map/zomq,qpy->zompy/dot_general | solution.py:237
  223.4 66.8 %reshape.480 = f32[4,1,131072]{2,1,0:T(1,128)S(1)} reshape(f32[512,8,8,2,8]{4,3,2,1,0:T(2,128)} %bitcast.185) | data formatting | bytes 4194304
  290.3 53.4 %all_to_all.63 = f32[4,1,131072]{2,1,0:T(1,128)} all-to-all(f32[4,1,131072]{2,1,0:T(1,128)S(1)} %reshape.480), channel_id=1, replica_groups=mesh['gx'=4,'gy'=4,'ga'=2] {'gy'}, dimensions={0} | all-to-all | bytes 4194304 | tf_op jit(solution)/shard_map/all_to_all | solution.py:243
  344.2 7.7 %reduce.8 = f32[4,131072]{1,0:T(4,128)S(1)} reduce(f32[4,1,131072]{2,1,0:T(1,128)} %all_to_all.63, f32[]{:T(128)} %broadcast.796), dimensions={1}, to_apply=%all_to_all.54.reduce_sub_computation | reduce | bytes 4194308 | tf_op jit(solution)/shard_map/all_to_all | solution.py:243
  351.9 65.7 %reshape.481 = f32[512,8,8,2,8]{4,3,2,1,0:T(2,128)} reshape(f32[4,131072]{1,0:T(4,128)S(1)} %reduce.8) | data formatting | bytes 4194304
  417.6 40.1 %copy.103 = f32[8,8,8,2,4,128]{5,2,4,3,1,0:T(8,128)S(1)} copy(f32[8,8,8,2,4,128]{2,3,1,0,5,4:T(2,128)} %bitcast.186) | data formatting | bytes 4194304 | tf_op jit(solution)/shard_map/all_to_all | solution.py:243
  457.7 1.1 fusion.16
  459.1 11.4 %all_to_all.64 = bf16[8,8,32,128]{3,1,0,2:T(8,128)(2,1)S(1)} all-to-all(bf16[8,8,32,128]{3,1,0,2:T(8,128)(2,1)S(1)} %copy.104), channel_id=1, replica_groups=mesh['gx'=4,'gy'=4,'ga'=2] {'gx'}, dimensions={2} | all-to-all | bytes 1048576 | tf_op jit(solution)/shard_map/all_to_all | solution.py:250
  (81 shorter events, 21.3 us)
Async XLA Ops:
  6.5 463.9 %copy-start = (bf16[32,32]{1,0:T(8,128)(2,1)S(1)}, bf16[32,32]{1,0:T(8,128)(2,1)}, u32[]{:S(2)}) copy-start(bf16[32,32]{1,0:T(8,128)(2,1)} %param.11) | copy-start | bytes 6148
  6.5 5.3 %copy-start.4 = (f32[5,8,16,256]{3,2,1,0:T(8,128)S(1)}, f32[5,8,16,256]{3,2,1,0:T(8,128)}, u32[]{:S(2)}) copy-start(f32[5,8,16,256]{3,2,1,0:T(8,128)} %param.7) | copy-start | bytes 1966084
  7.8 9.0 %collective-permute-start = (f32[6,8,3,256]{3,1,2,0:T(8,128)S(1)}, f32[6,8,3,256]{3,1,2,0:T(8,128)S(1)}, u32[]{:S(2)}, u32[]{:S(2)}) collective-permute-start(f32[6,8,3,256]{3,1,2,0:T(8,128)S(1)} %copy.159), channel_id=1, source_target_pairs={{0,8},{8,16},{16,24},{24,0},{1,9},{9,17},{17,25},{25,1},{2,10},{10... | collective-permute-start | bytes 442376 | tf_op jit(solution)/shard_map/ppermute | solution.py:23
  10.9 10.0 %collective-permute-start.1 = (f32[6,8,3,256]{3,1,2,0:T(8,128)S(1)}, f32[6,8,3,256]{3,1,2,0:T(8,128)S(1)}, u32[]{:S(2)}, u32[]{:S(2)}) collective-permute-start(f32[6,8,3,256]{3,1,2,0:T(8,128)S(1)} %copy.160), channel_id=1, source_target_pairs={{8,0},{16,8},{24,16},{0,24},{9,1},{17,9},{25,17},{1,25},{10,2},{18... | collective-permute-start | bytes 442376 | tf_op jit(solution)/shard_map/ppermute | solution.py:26
  24.8 8.7 %copy-start.2 = (f32[6,8,3,256]{2,1,3,0:T(8,128)S(1)}, f32[6,8,3,256]{2,1,3,0:T(8,128)}, u32[]{:S(2)}) copy-start(f32[6,8,3,256]{2,1,3,0:T(8,128)} %copy.87) | copy-start | bytes 442372
  26.2 7.0 %collective-permute-start.2 = (f32[6,8,22,3]{2,1,3,0:T(8,128)S(1)}, f32[6,8,22,3]{2,1,3,0:T(8,128)S(1)}, u32[]{:S(2)}, u32[]{:S(2)}) collective-permute-start(f32[6,8,22,3]{2,1,3,0:T(8,128)S(1)} %get-tuple-element.11), channel_id=1, source_target_pairs={{0,2},{2,4},{4,6},{6,0},{1,3},{3,5},{5,7},{7,1},{8,10},{10,12},{12... | collective-permute-start | bytes 38024 | tf_op jit(solution)/shard_map/ppermute | solution.py:23
  28.3 5.2 %collective-permute-start.3 = (f32[6,8,22,3]{2,1,3,0:T(8,128)S(1)}, f32[6,8,22,3]{2,1,3,0:T(8,128)S(1)}, u32[]{:S(2)}, u32[]{:S(2)}) collective-permute-start(f32[6,8,22,3]{2,1,3,0:T(8,128)S(1)} %get-tuple-element.12), channel_id=1, source_target_pairs={{2,0},{4,2},{6,4},{0,6},{3,1},{5,3},{7,5},{1,7},{10,8},{12,10},{14... | collective-permute-start | bytes 38024 | tf_op jit(solution)/shard_map/ppermute | solution.py:26
  40.0 3.7 copy-start.1
  47.8 7.9 %collective-permute-start.4 = (f32[6,3,22,262]{3,2,1,0:T(8,128)}, f32[6,3,22,262]{3,2,1,0:T(8,128)}, u32[]{:S(2)}, u32[]{:S(2)}) collective-permute-start(f32[6,3,22,262]{3,2,1,0:T(8,128)} %copy.88), channel_id=1, source_target_pairs={{0,1},{1,0},{2,3},{3,2},{4,5},{5,4},{6,7},{7,6},{8,9},{9,8},{10,11... | collective-permute-start | bytes 1245032 | tf_op jit(solution)/shard_map/ppermute | solution.py:23
  50.1 5.7 %collective-permute-start.5 = (f32[6,3,22,262]{3,2,1,0:T(8,128)}, f32[6,3,22,262]{3,2,1,0:T(8,128)S(1)}, u32[]{:S(2)}, u32[]{:S(2)}) collective-permute-start(f32[6,3,22,262]{3,2,1,0:T(8,128)} %copy.89), channel_id=1, source_target_pairs={{1,0},{0,1},{3,2},{2,3},{5,4},{4,5},{7,6},{6,7},{9,8},{8,9},{11,10... | collective-permute-start | bytes 1245032 | tf_op jit(solution)/shard_map/ppermute | solution.py:26
  89.5 1.2 copy-start.5
  89.5 1.2 copy-start.6
  93.0 11.9 %all-to-all-start = ((bf16[8,32,8,128]{3,2,0,1:T(8,128)(2,1)}), bf16[8,32,8,128]{3,2,0,1:T(8,128)(2,1)S(1)}, u32[]{:S(2)}, u32[]{:S(2)}) async-start(bf16[8,32,8,128]{3,2,0,1:T(8,128)(2,1)} %copy.94), calls=%async_computation | async-start | bytes 1048576 | tf_op jit(solution)/shard_map/all_to_all | solution.py:194
  105.8 18.2 %all-to-all-start.1 = ((bf16[8,8,32,128]{3,2,1,0:T(8,128)(2,1)}), bf16[8,8,32,128]{3,2,1,0:T(8,128)(2,1)S(1)}, u32[]{:S(2)}, u32[]{:S(2)}) async-start(bf16[8,8,32,128]{3,2,1,0:T(8,128)(2,1)} %bitcast.183), calls=%async_computation.1 | async-start | bytes 1048576 | tf_op jit(solution)/shard_map/all_to_all | solution.py:193
  110.3 60.4 %reduce-scatter.3.cloned.1.call-start = ((), (), s32[]{:S(2)}) async-start(), calls=%async_computation.6 | async-start | bytes 589824 | tf_op jit(solution)/shard_map/reduce_scatter | solution.py:220
  141.1 55.7 %reduce-scatter.5.cloned.1.call-start = ((), (), s32[]{:S(2)}) async-start(), calls=%async_computation.7 | async-start | bytes 786432 | tf_op jit(solution)/shard_map/reduce_scatter | solution.py:231
  181.7 2.2 copy-start.3
  457.7 12.7 %copy-start.7 = (f32[32]{0:T(128)S(1)}, f32[32]{0:T(128)}, u32[]{:S(2)}) copy-start(f32[32]{0:T(128)} %param.13) | copy-start | bytes 388
Sparse Core Ops, SparseCore 0:
  141.2 29.4 reduce-scatter.2
  191.0 5.7 reduce-scatter.4
where the time goes:
time: 483 us; the launch traced here: 479 us
  local copies, waits for them, and re-layouts  239 us (49%)
  blocking collectives  74.9 us (16%)
  waiting for transfers between devices  58.1 us (12%)
  other arithmetic  52.5 us (11%)
  matrix products  22.9 us (5%)
  starting transfers between devices  17.3 us (4%)
  between operations  14.2 us (3%)
    unnamed x32, local copies, waits for them, and re-layouts  136 us
    all_to_all x1, blocking collectives, shards(): lax.all_to_all(back_north, 'gy', split_axis=4, concat_axis=2, tiled=True)  53.4 us
    all_to_all x2, local copies, waits for them, and re-layouts, shards(): lax.all_to_all(back_north, 'gy', split_axis=4, concat_axis=2, tiled=True)  40.6 us
    reduce_scatter x1, waiting for transfers between devices, shards(): lax.psum_scatter(forward_depth_blocks(picked, depth_points, frequencies,...  29.5 us
    dot_general x1, local copies, waits for them, and re-layouts, shards(): jnp.einsum('zomq,qpy->zompy', back_depth, inverse_north_table(north_point...  23.9 us
    all_to_all x1, waiting for transfers between devices, shards(): lax.all_to_all(lax.all_to_all(lifted, 'gx', split_axis=1, concat_axis=2,...  11.9 us
    all_to_all x1, blocking collectives, shards(): lax.all_to_all(spectral, 'gx', split_axis=2, concat_axis=1, tiled=True)  11.4 us
    mul x1, other arithmetic, coarsen(): 0.25 * (blocks[:, :, :, 0, :, 0] + blocks[:, :, :, 1, :, 0] + blocks[:, :...  10.9 us
  transfers between devices with their start and end apart: 10, of which 6 were waited for; matrix products, arithmetic and copies ran while one was open for 4% of the time, Pallas kernels for 0%

commit v1 on v0

--- a/solution.py
+++ b/solution.py
@@ -240,7 +240,9 @@
         inverse_north_table(north_points, length_north, MY),
         precision=highest,
     )
-    all_modes = lax.all_to_all(back_north, "gy", split_axis=4, concat_axis=2, tiled=True)
+    cells = jnp.split(back_north, lax.axis_size("gy"), axis=4)
+    got = lax.all_to_all(jnp.stack(cells), "gy", 0, 0)
+    all_modes = jnp.concatenate(got, axis=2)
     spectral = jnp.einsum(
         "zompy,mpx->zoxy",
         all_modes,

time: 483 us -> 278 us (0.58)
  local copies, waits for them, and re-layouts: 239 us -> 42.6 us
  other arithmetic: 52.5 us -> 45 us
    unnamed x32 -> x30, local copies, waits for them, and re-layouts: 136 us -> 3.04 us
    all_to_all x2 -> x0, local copies, waits for them, and re-layouts: 40.6 us -> none  [shards(): lax.all_to_all(back_north, 'gy', split_axis=4, concat_axis=2, tiled=True)]
    dot_general x1 -> x0, local copies, waits for them, and re-layouts: 23.9 us -> none  [shards(): jnp.einsum('zomq,qpy->zompy', back_depth, inverse_north_table(north_point...]
    all_to_all x1 -> x0, other arithmetic: 7.72 us -> none  [shards(): lax.all_to_all(back_north, 'gy', split_axis=4, concat_axis=2, tiled=True)]
  transfers between devices with their start and end apart: 10 -> 10, of which waited for: 6 -> 6; matrix products, arithmetic and copies ran while one was open for 4% -> 7% of each run, Pallas kernels for 0% -> 0%
where the time goes in v1:
time: 278 us; the launch traced here: 275 us
  blocking collectives  74.9 us (27%)
  waiting for transfers between devices  57.6 us (21%)
  other arithmetic  45 us (16%)
  local copies, waits for them, and re-layouts  42.6 us (15%)
  matrix products  22.9 us (8%)
  starting transfers between devices  17.8 us (6%)
  between operations  14.1 us (5%)
    all_to_all x1, blocking collectives, shards(): got = lax.all_to_all(jnp.stack(cells), 'gy', 0, 0)  53.3 us
    reduce_scatter x1, waiting for transfers between devices, shards(): lax.psum_scatter(forward_depth_blocks(picked, depth_points, frequencies,...  29.4 us
    all_to_all x1, waiting for transfers between devices, shards(): lax.all_to_all(lax.all_to_all(lifted, 'gx', split_axis=1, concat_axis=2,...  11.9 us
    all_to_all x1, blocking collectives, shards(): lax.all_to_all(spectral, 'gx', split_axis=2, concat_axis=1, tiled=True)  11.4 us
    mul x1, other arithmetic, coarsen(): 0.25 * (blocks[:, :, :, 0, :, 0] + blocks[:, :, :, 1, :, 0] + blocks[:, :...  10.9 us
    all_gather x1, blocking collectives, shards(): lax.all_gather(coeffs, 'gx', axis=1, tiled=True)  10.2 us
    add x3, other arithmetic, step_interior(): center - courant_half * (transport + coupling) + smooth_half * curvature  8.56 us
    all_to_all x1, waiting for transfers between devices, shards(): lax.all_to_all(lifted, 'gx', split_axis=1, concat_axis=2, tiled=True)  8.4 us
  transfers between devices with their start and end apart: 10, of which 6 were waited for; matrix products, arithmetic and copies ran while one was open for 7% of the time, Pallas kernels for 0%

profile of v1, /device:TPU:0, one launch (start us, length us, event | category | flops | bytes accessed | tf_op | source)
XLA Modules:
  0.0 274.9 jit_solution(11484271271268144863)
XLA Ops:
  6.5 1.2 fusion.68
  7.8 3.0 %collective-permute-start = (f32[6,8,3,256]{3,1,2,0:T(8,128)S(1)}, f32[6,8,3,256]{3,1,2,0:T(8,128)S(1)}, u32[]{:S(2)}, u32[]{:S(2)}) collective-permute-start(f32[6,8,3,256]{3,1,2,0:T(8,128)S(1)} %copy.154), channel_id=1, source_target_pairs={{0,8},{8,16},{16,24},{24,0},{1,9},{9,17},{17,25},{25,1},{2,10},{10... | collective-permute-start | bytes 442376 | tf_op jit(solution)/shard_map/ppermute | solution.py:23
  10.9 1.0 collective-permute-start.1
  11.9 1.0 pad_maximum_fusion.3
  12.9 4.0 %copy.84 = f32[6,8,16,256]{2,1,3,0:T(8,128)} copy(f32[6,8,16,256]{3,2,1,0:T(8,128)S(1)} %pad_maximum_fusion.3) | data formatting | bytes 1572864 | tf_op jit(solution)/shard_map/concatenate | solution.py:174
  16.8 4.0 %copy.83 = f32[6,8,3,256]{2,1,3,0:T(8,128)} copy(f32[6,8,3,256]{3,1,2,0:T(8,128)S(1)} %collective-permute-done) | data formatting | bytes 294912 | tf_op jit(solution)/shard_map/ppermute | solution.py:23
  20.9 4.0 %copy.85 = f32[6,8,3,256]{2,1,3,0:T(8,128)} copy(f32[6,8,3,256]{3,1,2,0:T(8,128)S(1)} %collective-permute-done.1) | data formatting | bytes 294912 | tf_op jit(solution)/shard_map/ppermute | solution.py:26
  24.9 1.4 pad_maximum_fusion.8
  26.3 2.1 collective-permute-start.2
  28.3 2.6 collective-permute-start.3
  30.9 2.1 collective-permute-done.2
  33.6 6.5 %pad_maximum_fusion = f32[6,8,22,262]{2,1,3,0:T(8,128)S(1)} fusion(f32[6,8,22,3]{2,1,3,0:T(8,128)S(1)} %collective-permute-done.3, f32[6,8,3,256]{2,1,3,0:T(8,128)S(1)} %copy-done.2, f32[6,8,16,256]{2,1,3,0:T(8,128)} %copy.84, f32[6,8,3,256]{2,1,3,0:T(8,128)} %copy.83, f32[6,8,22,3]{2,1,3,0:T(8,128)S(1)} %collective-permute-done.2), kind=kLoop, calls=%fused_computation.1 | loop fusion | flops 1106688 | bytes 2213376 | tf_op jit(solution)/shard_map/concatenate | solution.py:27
  40.1 3.2 %fusion.168 = (f32[6,3,22,262]{2,1,3,0:T(4,128)}, f32[6,3,22,262]{2,1,3,0:T(4,128)S(1)}) fusion(f32[6,8,22,262]{2,1,3,0:T(8,128)S(1)} %pad_maximum_fusion), kind=kLoop, calls=%fused_computation.279 | loop fusion | bytes 1660032 | tf_op jit(solution)/shard_map/slice | solution.py:24
  43.8 4.0 %copy.86 = f32[6,3,22,262]{3,2,1,0:T(8,128)} copy(f32[6,3,22,262]{2,1,3,0:T(4,128)} %get-tuple-element.13) | data formatting | bytes 830016 | tf_op jit(solution)/shard_map/slice | solution.py:24
  47.9 2.3 copy.87
  50.7 5.1 %copy.88 = f32[6,8,22,262]{3,2,1,0:T(8,128)S(1)} copy(f32[6,8,22,262]{2,1,3,0:T(8,128)} %copy-done.1) | data formatting | bytes 2213376 | tf_op jit(solution)/shard_map/concatenate | solution.py:27
  55.8 1.3 pad_maximum_fusion.1
  57.1 3.0 %slice_subtract_fusion.2 = (f32[5,12,20,260]{3,2,1,0:T(8,128)S(1)}, f32[5,12,20,260]{3,2,1,0:T(8,128)S(1)}, f32[5,12,20,260]{3,2,1,0:T(8,128)S(1)}) fusion(f32[6,14,22,262]{3,2,1,0:T(8,128)S(1)} %pad_maximum_fusion.1), kind=kLoop, calls=%fused_computation.20 | loop fusion | flops 936000 | bytes 11232000 | tf_op jit(solution)/shard_map/sub | solution.py:40
  60.6 4.1 %multiply_add_fusion = f32[5,12,20,260]{3,2,1,0:T(8,128)S(1)} fusion(f32[6,14,22,262]{3,2,1,0:T(8,128)S(1)} %pad_maximum_fusion.1, f32[5,12,20,260]{3,2,1,0:T(8,128)S(1)} %fusion.52, f32[5,12,20,260]{3,2,1,0:T(8,128)S(1)} %get-tuple-element.17, f32[5,12,20,260]{3,2,1,0:T(8,128)S(1)} %get-tuple-element.16, f32[5,12,20,260]{3,2,1,0:T(8,128)S(1)} %get-tuple-element.15), kind=kLoop, calls=%fused_computation.11 | loop fusion | flops 5304000 | bytes 14976000 | tf_op jit(solution)/shard_map/add | solution.py:56
  64.6 2.5 slice_subtract_fusion.5
  67.5 3.3 %multiply_add_fusion.1 = f32[5,10,18,258]{3,2,1,0:T(8,128)S(1)} fusion(f32[5,12,20,260]{3,2,1,0:T(8,128)S(1)} %multiply_add_fusion, f32[5,10,18,258]{3,2,1,0:T(8,128)S(1)} %fusion.60, f32[5,10,18,258]{3,2,1,0:T(8,128)S(1)} %get-tuple-element.19, f32[5,10,18,258]{3,2,1,0:T(8,128)S(1)} %get-tuple-element.20, f32[5,10,18,258]{3,2,1,0:T(8,128)S(1)} %get-tuple-element.18), kind=kLoop, calls=%fused_computation.21 | loop fusion | flops 3947400 | bytes 11145600 | tf_op jit(solution)/shard_map/add | solution.py:56
  71.9 1.2 multiply_add_fusion.2
  73.1 5.5 %copy.89 = f32[5,8,16,256]{1,3,2,0:T(8,128)} copy(f32[5,8,16,256]{3,2,1,0:T(8,128)S(1)} %multiply_add_fusion.2) | data formatting | bytes 1310720 | tf_op jit(solution)/shard_map/add | solution.py:56
  78.6 10.9 %fusion = f32[5,8,8,1,128,1]{1,5,4,3,2,0:T(1,128)S(1)} fusion(f32[5,8,8,2,128,2]{1,5,4,3,2,0:T(2,128)} %bitcast.188), kind=kLoop, calls=%fused_computation.8 | loop fusion | flops 163840 | bytes 819200 | tf_op jit(solution)/shard_map/mul | solution.py:66
  89.6 1.1 copy.90
  90.7 1.3 fusion.30
  92.1 1.0 copy.92
  93.1 3.5 %all-to-all-start = ((bf16[8,32,8,128]{3,2,0,1:T(8,128)(2,1)}), bf16[8,32,8,128]{3,2,0,1:T(8,128)(2,1)S(1)}, u32[]{:S(2)}, u32[]{:S(2)}) async-start(bf16[8,32,8,128]{3,2,0,1:T(8,128)(2,1)} %copy.92), calls=%async_computation | async-start | bytes 1048576 | tf_op jit(solution)/shard_map/all_to_all | solution.py:194
  96.6 8.4 %all-to-all-done = bf16[8,32,8,128]{3,2,0,1:T(8,128)(2,1)S(1)} async-done(((bf16[8,32,8,128]{3,2,0,1:T(8,128)(2,1)}), bf16[8,32,8,128]{3,2,0,1:T(8,128)(2,1)S(1)}, u32[]{:S(2)}, u32[]{:S(2)}) %all-to-all-start) | async-done | bytes 524320 | tf_op jit(solution)/shard_map/all_to_all | solution.py:194
  105.9 4.7 %all-to-all-start.1 = ((bf16[8,8,32,128]{3,2,1,0:T(8,128)(2,1)}), bf16[8,8,32,128]{3,2,1,0:T(8,128)(2,1)S(1)}, u32[]{:S(2)}, u32[]{:S(2)}) async-start(bf16[8,8,32,128]{3,2,1,0:T(8,128)(2,1)} %bitcast.186), calls=%async_computation.1 | async-start | bytes 1048576 | tf_op jit(solution)/shard_map/all_to_all | solution.py:193
  111.0 1.1 fusion.84
  112.5 11.9 %all-to-all-done.1 = bf16[8,8,32,128]{3,2,1,0:T(8,128)(2,1)S(1)} async-done(((bf16[8,8,32,128]{3,2,1,0:T(8,128)(2,1)}), bf16[8,8,32,128]{3,2,1,0:T(8,128)(2,1)S(1)}, u32[]{:S(2)}, u32[]{:S(2)}) %all-to-all-start.1) | async-done | bytes 524320 | tf_op jit(solution)/shard_map/all_to_all | solution.py:193
  125.6 1.8 fusion.20
  128.6 2.4 fusion.57
  131.0 3.0 %fusion.53 = f32[8,4,8,8,64]{4,1,3,2,0:T(4,128)S(1)} fusion(f32[2,8,8,8,128]{4,0,3,1,2:T(2,128)S(1)} %fusion.50, s32[8,4]{1,0:T(8,128)S(1)} %iota_add_fusion, s32[2]{0:T(128)S(1)} %iota_add_fusion.2), kind=kOutput, calls=%fused_computation.101 | convolution fusion | flops 3146688 | bytes 1048712 | tf_op jit(solution)/shard_map/zcrbn,rkz->rkcbn/dot_general | solution.py:132
  133.9 3.3 %fusion.15 = bf16[8,4,8,8,64]{4,1,3,2,0:T(4,128)(2,1)S(1)} fusion(f32[8,4,8,8,64]{4,1,3,2,0:T(4,128)S(1)} %fusion.57, f32[2,8,8,8,128]{4,0,3,1,2:T(2,128)S(1)} %fusion.50, s32[8,4]{1,0:T(8,128)S(1)} %iota_add_fusion, s32[2]{0:T(128)S(1)} %iota_add_fusion.2), kind=kOutput, calls=%fused_computation.39 | convolution fusion | flops 3408832 | bytes 1310856 | tf_op jit(solution)/shard_map/zcrbn,rkz->rkcbn/dot_general | solution.py:129
  137.2 2.5 fusion.16
  141.5 29.4 %reduce-scatter.3.cloned.1.call-done = bf16[1,4,8,8,128]{4,3,2,1,0:T(8,128)(2,1)} async-done(((bf16[8,4,8,8,128]{4,3,2,1,0:T(8,128)(2,1)}), bf16[1,4,8,8,128]{4,3,2,1,0:T(8,128)(2,1)}) %reduce-scatter.3.cloned.1.call-update) | async-done | bytes 65552 | tf_op jit(solution)/shard_map/reduce_scatter | solution.py:220
  171.8 10.2 %all-gather = f32[1,4,32,8,128]{4,3,1,0,2:T(8,128)S(1)} all-gather(f32[1,4,8,8,128]{4,3,1,0,2:T(8,128)S(1)} %copy.98), channel_id=2, replica_groups=mesh['gx'=4,'gy'=4,'ga'=2] {'gx'}, dimensions={2}, use_global_device_ids=true | all-gather | bytes 655360 | tf_op jit(solution)/shard_map/all_gather | solution.py:226
  182.8 1.3 copy-done.3
  184.2 2.4 multiply_reduce_fusion.3
  190.1 1.0 pad_maximum_fusion.5
  191.8 5.1 %reduce-scatter.5.cloned.1.call-done = f32[8,8,8,128]{3,0,2,1:T(8,128)} async-done(((f32[16,8,8,128]{3,0,2,1:T(8,128)}), f32[8,8,8,128]{3,0,2,1:T(8,128)}) %reduce-scatter.5.cloned.1.call-update) | async-done | bytes 262160 | tf_op jit(solution)/shard_map/reduce_scatter | solution.py:231
  196.9 2.7 fusion.41
  200.2 53.3 %all_to_all.50 = f32[4,8,8,8,2,128]{5,3,4,2,1,0:T(8,128)S(1)} all-to-all(f32[4,8,8,8,2,128]{5,3,4,2,1,0:T(8,128)S(1)} %pad_maximum_fusion.2), channel_id=1, replica_groups=mesh['gx'=4,'gy'=4,'ga'=2] {'gy'}, dimensions={0} | all-to-all | bytes 4194304 | tf_op jit(solution)/shard_map/all_to_all | solution.py:244
  253.5 1.1 fusion.17
  254.8 11.4 %all_to_all.51 = bf16[8,8,32,128]{3,1,0,2:T(8,128)(2,1)S(1)} all-to-all(bf16[8,8,32,128]{3,1,0,2:T(8,128)(2,1)S(1)} %copy.101), channel_id=1, replica_groups=mesh['gx'=4,'gy'=4,'ga'=2] {'gx'}, dimensions={2} | all-to-all | bytes 1048576 | tf_op jit(solution)/shard_map/all_to_all | solution.py:252
  266.9 1.0 copy.103
  (77 shorter events, 16.5 us)
Async XLA Ops:
  6.5 259.7 %copy-start = (bf16[32,32]{1,0:T(8,128)(2,1)S(1)}, bf16[32,32]{1,0:T(8,128)(2,1)}, u32[]{:S(2)}) copy-start(bf16[32,32]{1,0:T(8,128)(2,1)} %param.11) | copy-start | bytes 6148
  6.5 5.3 %copy-start.4 = (f32[5,8,16,256]{3,2,1,0:T(8,128)S(1)}, f32[5,8,16,256]{3,2,1,0:T(8,128)}, u32[]{:S(2)}) copy-start(f32[5,8,16,256]{3,2,1,0:T(8,128)} %param.7) | copy-start | bytes 1966084
  7.8 9.0 %collective-permute-start = (f32[6,8,3,256]{3,1,2,0:T(8,128)S(1)}, f32[6,8,3,256]{3,1,2,0:T(8,128)S(1)}, u32[]{:S(2)}, u32[]{:S(2)}) collective-permute-start(f32[6,8,3,256]{3,1,2,0:T(8,128)S(1)} %copy.154), channel_id=1, source_target_pairs={{0,8},{8,16},{16,24},{24,0},{1,9},{9,17},{17,25},{25,1},{2,10},{10... | collective-permute-start | bytes 442376 | tf_op jit(solution)/shard_map/ppermute | solution.py:23
  10.9 10.0 %collective-permute-start.1 = (f32[6,8,3,256]{3,1,2,0:T(8,128)S(1)}, f32[6,8,3,256]{3,1,2,0:T(8,128)S(1)}, u32[]{:S(2)}, u32[]{:S(2)}) collective-permute-start(f32[6,8,3,256]{3,1,2,0:T(8,128)S(1)} %copy.155), channel_id=1, source_target_pairs={{8,0},{16,8},{24,16},{0,24},{9,1},{17,9},{25,17},{1,25},{10,2},{18... | collective-permute-start | bytes 442376 | tf_op jit(solution)/shard_map/ppermute | solution.py:26
  24.9 8.7 %copy-start.2 = (f32[6,8,3,256]{2,1,3,0:T(8,128)S(1)}, f32[6,8,3,256]{2,1,3,0:T(8,128)}, u32[]{:S(2)}) copy-start(f32[6,8,3,256]{2,1,3,0:T(8,128)} %copy.85) | copy-start | bytes 442372
  26.3 6.8 %collective-permute-start.2 = (f32[6,8,22,3]{2,1,3,0:T(8,128)S(1)}, f32[6,8,22,3]{2,1,3,0:T(8,128)S(1)}, u32[]{:S(2)}, u32[]{:S(2)}) collective-permute-start(f32[6,8,22,3]{2,1,3,0:T(8,128)S(1)} %get-tuple-element.11), channel_id=1, source_target_pairs={{0,2},{2,4},{4,6},{6,0},{1,3},{3,5},{5,7},{7,1},{8,10},{10,12},{12... | collective-permute-start | bytes 38024 | tf_op jit(solution)/shard_map/ppermute | solution.py:23
  28.3 5.2 %collective-permute-start.3 = (f32[6,8,22,3]{2,1,3,0:T(8,128)S(1)}, f32[6,8,22,3]{2,1,3,0:T(8,128)S(1)}, u32[]{:S(2)}, u32[]{:S(2)}) collective-permute-start(f32[6,8,22,3]{2,1,3,0:T(8,128)S(1)} %get-tuple-element.12), channel_id=1, source_target_pairs={{2,0},{4,2},{6,4},{0,6},{3,1},{5,3},{7,5},{1,7},{10,8},{12,10},{14... | collective-permute-start | bytes 38024 | tf_op jit(solution)/shard_map/ppermute | solution.py:26
  40.1 3.7 %copy-start.1 = (f32[6,8,22,262]{2,1,3,0:T(8,128)}, f32[6,8,22,262]{2,1,3,0:T(8,128)S(1)}, u32[]{:S(2)}) copy-start(f32[6,8,22,262]{2,1,3,0:T(8,128)S(1)} %pad_maximum_fusion) | copy-start | bytes 3320068
  47.9 7.9 %collective-permute-start.4 = (f32[6,3,22,262]{3,2,1,0:T(8,128)}, f32[6,3,22,262]{3,2,1,0:T(8,128)}, u32[]{:S(2)}, u32[]{:S(2)}) collective-permute-start(f32[6,3,22,262]{3,2,1,0:T(8,128)} %copy.86), channel_id=1, source_target_pairs={{0,1},{1,0},{2,3},{3,2},{4,5},{5,4},{6,7},{7,6},{8,9},{9,8},{10,11... | collective-permute-start | bytes 1245032 | tf_op jit(solution)/shard_map/ppermute | solution.py:23
  50.2 5.7 %collective-permute-start.5 = (f32[6,3,22,262]{3,2,1,0:T(8,128)}, f32[6,3,22,262]{3,2,1,0:T(8,128)S(1)}, u32[]{:S(2)}, u32[]{:S(2)}) collective-permute-start(f32[6,3,22,262]{3,2,1,0:T(8,128)} %copy.87), channel_id=1, source_target_pairs={{1,0},{0,1},{3,2},{2,3},{5,4},{4,5},{7,6},{6,7},{9,8},{8,9},{11,10... | collective-permute-start | bytes 1245032 | tf_op jit(solution)/shard_map/ppermute | solution.py:26
  89.5 1.2 copy-start.5
  89.5 1.2 copy-start.6
  93.1 11.9 %all-to-all-start = ((bf16[8,32,8,128]{3,2,0,1:T(8,128)(2,1)}), bf16[8,32,8,128]{3,2,0,1:T(8,128)(2,1)S(1)}, u32[]{:S(2)}, u32[]{:S(2)}) async-start(bf16[8,32,8,128]{3,2,0,1:T(8,128)(2,1)} %copy.92), calls=%async_computation | async-start | bytes 1048576 | tf_op jit(solution)/shard_map/all_to_all | solution.py:194
  105.9 18.5 %all-to-all-start.1 = ((bf16[8,8,32,128]{3,2,1,0:T(8,128)(2,1)}), bf16[8,8,32,128]{3,2,1,0:T(8,128)(2,1)S(1)}, u32[]{:S(2)}, u32[]{:S(2)}) async-start(bf16[8,8,32,128]{3,2,1,0:T(8,128)(2,1)} %bitcast.186), calls=%async_computation.1 | async-start | bytes 1048576 | tf_op jit(solution)/shard_map/all_to_all | solution.py:193
  110.6 60.3 %reduce-scatter.3.cloned.1.call-start = ((), (), s32[]{:S(2)}) async-start(), calls=%async_computation.6 | async-start | bytes 589824 | tf_op jit(solution)/shard_map/reduce_scatter | solution.py:220
  141.4 55.5 %reduce-scatter.5.cloned.1.call-start = ((), (), s32[]{:S(2)}) async-start(), calls=%async_computation.7 | async-start | bytes 786432 | tf_op jit(solution)/shard_map/reduce_scatter | solution.py:231
  182.0 2.2 copy-start.3
  253.5 12.7 %copy-start.7 = (f32[32]{0:T(128)S(1)}, f32[32]{0:T(128)}, u32[]{:S(2)}) copy-start(f32[32]{0:T(128)} %param.13) | copy-start | bytes 388
Sparse Core Ops, SparseCore 0:
  141.6 29.2 reduce-scatter.2
  191.3 5.5 reduce-scatter.4
